TPU v7x, 32 devices: a whole 2x2x4 slice. The times are simulated.
32 devices in a mesh: groups: 2 (over x), wide: 16 (over z, y, core).
Axes of the slice: x: 2, y: 2, z: 4, core: 2. Of those that a mesh axis runs over, the one named last changes fastest.
Arguments:
- residual: bfloat16 [4096, 2048], P(('groups', 'wide')), parts along dimension 0, may hold values from -6 to 6
- queries: bfloat16 [4096, 2048], P(('groups', 'wide')), parts along dimension 0, may hold values from -160 to 160
- new_keys: bfloat16 [4096, 256], P(('groups', 'wide')), parts along dimension 0, may hold values from -6 to 6
- new_values: bfloat16 [4096, 256], P(('groups', 'wide')), parts along dimension 0, may hold values from -6 to 6
- cache_keys: bfloat16 [32, 2048, 256], P(('groups', 'wide')), parts along dimension 0, may hold values from -6 to 6
- cache_values: bfloat16 [32, 2048, 256], P(('groups', 'wide')), parts along dimension 0, may hold values from -6 to 6
- cache_len: int32 [32], P('groups'), parts along dimension 0, may hold values from 1 to 2048, 16384 in all
- o_weight: bfloat16 [2048, 2048], P('wide'), may hold values from -0.75 to 0.75
- norm_gain: float32 [2048], replicated, may hold values from 0.5 to 2
- expert_ids: int32 [4096, 8], P(('groups', 'wide')), parts along dimension 0, may hold values from 0 to 15, all different within a row; in each aligned block of 128 rows (0 to 127, 128 to 255, ...) at most 72 rows name the same one
- gate_raw: float32 [4096, 8], P(('groups', 'wide')), parts along dimension 0, may hold values from 0.1 to 1
- w_gate: bfloat16 [16, 2048, 768], P('wide'), may hold values from -0.125 to 0.125
- w_up: bfloat16 [16, 2048, 768], P('wide'), may hold values from -0.125 to 0.125
- w_down: bfloat16 [16, 768, 2048], P('wide'), may hold values from -0.4375 to 0.4375
Outputs:
- layer_out: bfloat16 [4096, 2048], P(('groups', 'wide')), parts along dimension 0
There are 2 independent parts, one for each index of `groups`. A program takes and returns all parts, laid end to end along the dimension named above; an argument that names none is the same for every part. Nothing has to cross between parts.
Inputs may be any that keep to these rules, and one draw needn't show every extreme that they name: `cache_len`: each span's cache holds 1 or more positions; in every part some span has a full cache of 2048 positions and the lengths sum to 16384. `expert_ids`: each token names 8 different experts; among the 128 tokens of one span no expert is named more than 72 times, and in every draw some span names some expert exactly 72 times.
All inputs are finite; a program needn't handle non-finite values.
Results may differ from a plain program's by a relative error of at most 0.01.
Values may be sent and summed in bfloat16 or wider, within the bound.
A program may use at most 128 MiB of HBM per device.

v0:
```python
import jax
import jax.numpy as jnp
from jax import lax
from jax.sharding import PartitionSpec as P

D = 2048
HEADS = 16
KV_HEADS = 2
HEAD = 128
TOPK = 8
KEY_BLOCK = 512
SPAN = 128


def group_queries(query_rows):
    return query_rows.reshape(query_rows.shape[0], KV_HEADS, HEADS // KV_HEADS, HEAD)


def empty_state(token_count):
    shape = (KV_HEADS, HEADS // KV_HEADS, token_count)
    return (
        jnp.full(shape, -1e30, jnp.float32),
        jnp.zeros(shape, jnp.float32),
        jnp.zeros(shape + (HEAD,), jnp.float32),
    )


def update(state, query_four, key_block, value_block, visible):
    run_max, run_total, run_acc = state
    key_three = key_block.reshape(-1, KV_HEADS, HEAD)
    value_three = value_block.reshape(-1, KV_HEADS, HEAD)
    scores = jnp.einsum(
        "tgrd,kgd->grtk", query_four, key_three, preferred_element_type=jnp.float32
    ) * HEAD ** (-0.5)
    scores = jnp.where(visible[None, None], scores, jnp.float32(-1e30))
    new_max = jnp.maximum(run_max, jnp.max(scores, axis=-1))
    rescale = jnp.exp(run_max - new_max)
    weights = jnp.exp(scores - new_max[..., None])
    run_total = run_total * rescale + jnp.sum(weights, axis=-1)
    run_acc = run_acc * rescale[..., None] + jnp.einsum(
        "grtk,kgd->grtd",
        weights.astype(jnp.bfloat16),
        value_three,
        preferred_element_type=jnp.float32,
    )
    return (new_max, run_total, run_acc)


def cache_pass(state, query_four, key_rows, value_rows, length, offset, block_count):
    token_count = query_four.shape[0]

    def block_step(block, carried):
        first_row = block * KEY_BLOCK
        key_block = lax.dynamic_slice_in_dim(key_rows, first_row, KEY_BLOCK, 0)
        value_block = lax.dynamic_slice_in_dim(value_rows, first_row, KEY_BLOCK, 0)
        positions = offset + first_row + jnp.arange(KEY_BLOCK, dtype=jnp.int32)
        visible = jnp.broadcast_to((positions < length)[None, :], (token_count, KEY_BLOCK))
        return update(carried, query_four, key_block, value_block, visible)

    return lax.fori_loop(0, block_count, block_step, state)


def run_expert(rows_in, gate_w, up_w, down_w):
    flat_rows = rows_in.reshape(-1, rows_in.shape[-1])
    gate_part = jnp.dot(flat_rows, gate_w, preferred_element_type=jnp.float32)
    up_part = jnp.dot(flat_rows, up_w, preferred_element_type=jnp.float32)
    activated = (jax.nn.silu(gate_part) * up_part).astype(jnp.bfloat16)
    expert_rows = jnp.dot(activated, down_w, preferred_element_type=jnp.float32).astype(
        jnp.bfloat16
    )
    return expert_rows.reshape(rows_in.shape)


def per_device(
    residual,
    queries,
    new_keys,
    new_values,
    cache_keys,
    cache_values,
    cache_len,
    o_weight,
    norm_gain,
    expert_ids,
    gate_raw,
    w_gate,
    w_up,
    w_down,
):
    devices = lax.axis_size("wide")
    my_index = lax.axis_index("wide")
    token_count = queries.shape[0]
    query_four = group_queries(queries)
    key_cache = cache_keys[0]
    value_cache = cache_values[0]
    length = cache_len[my_index]
    own_blocks = (length + KEY_BLOCK - 1) // KEY_BLOCK
    token_rows = jnp.arange(token_count, dtype=jnp.int32)
    causal = token_rows[None, :] <= token_rows[:, None]
    state = update(empty_state(token_count), query_four, new_keys, new_values, causal)
    state = cache_pass(state, query_four, key_cache, value_cache, length, 0, own_blocks)
    attn_four = state[2] / state[1][..., None]
    attn = (
        jnp.transpose(attn_four, (2, 0, 1, 3))
        .reshape(token_count, HEADS * HEAD)
        .astype(jnp.bfloat16)
    )
    projected = jnp.dot(
        attn,
        lax.all_gather(o_weight, "wide", axis=0, tiled=True),
        preferred_element_type=jnp.float32,
    )
    mixed = residual.astype(jnp.float32) + projected
    normed = (
        mixed * lax.rsqrt(jnp.mean(mixed * mixed, axis=-1, keepdims=True) + 1e-06) * norm_gain
    ).astype(jnp.bfloat16)
    capacity = SPAN * TOPK // devices + max(2, SPAN * TOPK // (8 * devices))
    flat_ids = expert_ids.reshape(-1)
    one_hot = (flat_ids[:, None] == jnp.arange(devices, dtype=jnp.int32)[None, :]).astype(jnp.int32)
    ranks = jnp.sum(jnp.cumsum(one_hot, axis=0) * one_hot, axis=1) - 1
    slot_index = flat_ids * capacity + ranks
    token_of = jnp.arange(flat_ids.shape[0], dtype=jnp.int32) // TOPK
    slot_token = (
        jnp.full((devices * capacity,), token_count, jnp.int32).at[slot_index].set(token_of)
    )
    padded = jnp.concatenate([normed, jnp.zeros((1, D), jnp.bfloat16)], axis=0)
    outgoing = padded[slot_token].reshape(devices, capacity, D)
    arrived = lax.all_to_all(outgoing, "wide", split_axis=0, concat_axis=0, tiled=True)
    served = run_expert(arrived, w_gate[0], w_up[0], w_down[0])
    returned_rows = lax.all_to_all(served, "wide", split_axis=0, concat_axis=0, tiled=True)
    picked = returned_rows.reshape(devices * capacity, D)[slot_index].reshape(token_count, TOPK, D)
    shares = gate_raw / jnp.sum(gate_raw, axis=-1, keepdims=True)
    routed = jnp.sum(picked.astype(jnp.float32) * shares[..., None], axis=1)
    return (mixed + routed).astype(jnp.bfloat16)


def solution(mesh):
    placed = (
        P(("groups", "wide"), None),
        P(("groups", "wide"), None),
        P(("groups", "wide"), None),
        P(("groups", "wide"), None),
        P(("groups", "wide"), None, None),
        P(("groups", "wide"), None, None),
        P("groups"),
        P("wide", None),
        P(),
        P(("groups", "wide"), None),
        P(("groups", "wide"), None),
        P("wide", None, None),
        P("wide", None, None),
        P("wide", None, None),
    )
    return jax.shard_map(
        per_device,
        mesh=mesh,
        in_specs=placed,
        out_specs=P(("groups", "wide"), None),
        check_vma=False,
    )
```

profile of v0, /device:TPU:13, one launch (start us, length us, event | category | flops | bytes accessed | tf_op | source)
XLA Modules:
  0.0 360.3 jit_solution(6615246310391238780)
XLA Ops:
  6.5 0.7 all-gather.2.cloned.1.call-update
  7.3 1.5 dynamic_slice.9
  9.5 0.8 copy.35
  10.5 2.0 copy.25
  12.5 0.9 reshape.116
  13.4 0.9 reshape.118
  14.2 2.0 copy.32
  16.3 2.3 copy.30
  18.6 2.3 copy.31
  20.9 1.3 fusion.37
  22.5 1.5 convolution_add_fusion.1
  24.0 22.6 %while.14 = (s32[]{:T(128)}, f32[2,8,128]{2,1,0:T(8,128)S(1)}, f32[2,8,128]{2,1,0:T(8,128)S(1)}, f32[2,8,128,128]{3,2,1,0:T(8,128)}, s32[]{:T(128)}, /*index=5*/...) while((s32[]{:T(128)}, f32[2,8,128]{2,1,0:T(8,128)S(1)}, ...), condition=%wide.region_5.6_spmd, body=%wide.region_2.5_spmd.sunk | while | flops 548934656 | bytes 25299184 | solution.py:60
  24.0 1.1 constant_dynamic-slice_fusion.3
  25.1 0.7 add_compare_fusion.2
  25.7 2.2 bitcast_reduce_fusion.2
  28.0 0.9 fusion.57
  28.9 1.6 fusion.58
  30.5 1.0 copy-done.4
  31.5 1.1 constant_dynamic-slice_fusion.3
  32.6 0.7 add_compare_fusion.2
  33.3 2.2 bitcast_reduce_fusion.2
  35.5 0.9 fusion.57
  36.4 1.6 fusion.58
  38.0 1.0 copy-done.4
  39.0 1.1 constant_dynamic-slice_fusion.3
  40.1 0.7 add_compare_fusion.2
  40.8 2.2 bitcast_reduce_fusion.2
  43.0 0.9 fusion.57
  43.9 1.6 fusion.58
  45.6 1.0 copy-done.4
  46.5 2.6 copy.33
  49.2 4.5 %reduce-window.6 = s32[16,8,128]{2,1,0:T(8,128)S(1)} reduce-window(s32[16,8,128]{2,1,0:T(8,128)S(1)} %fusion.30, s32[]{:T(128)} %constant.46.clone.1), window={size=1x1x128 pad=0_0x0_0x127_0}, to_apply=%region_7.8 | reduce-window | flops 2080768 | bytes 131076 | tf_op jit(solution)/shard_map/reduce-window
  54.4 4.3 %scatter_custom_fusion = s32[1152]{0:T(1024)S(1)} fusion(s32[1024]{0:T(1024)S(1)} %bitcast.107, s32[1024]{0:T(1024)S(1)} %add_select_fusion, s32[]{:T(128)} %constant.87.clone.1), kind=kCustom, calls=%fused_computation.64 | custom fusion | bytes 4612 | tf_op jit(solution)/shard_map/scatter | solution.py:124
  58.7 2.2 divide_convert_fusion
  60.9 23.3 %all-gather.2.cloned.1.call-done = bf16[2048,2048]{1,0:T(8,128)(2,1)} async-done(((bf16[128,2048]{1,0:T(8,128)(2,1)}), bf16[2048,2048]{1,0:T(8,128)(2,1)}) %all-gather.2.cloned.1.call-update) | async-done | bytes 8388624 | tf_op jit(solution)/shard_map/all_gather | solution.py:110
  84.2 4.9 %multiply_reduce_fusion = (f32[128]{0:T(128)S(1)}, f32[128,2048]{1,0:T(8,128)S(1)}) fusion(bf16[128,2048]{0,1:T(8,128)(2,1)} %bitcast.102, bf16[2048,2048]{1,0:T(8,128)(2,1)} %all-gather.2.cloned.1.call-done, bf16[128,2048]{1,0:T(8,128)(2,1)} %param.16), kind=kOutput, calls=%fused_computation.38 | convolution fusion | flops 1074790272 | bytes 10486272 | tf_op jit(solution)/shard_map/dot_general | solution.py:108
  89.2 1.0 copy-done.1
  90.3 0.9 concatenate.3
  91.2 11.8 %gather_fusion = bf16[1152,2048]{1,0:T(8,128)(2,1)} fusion(bf16[129,2048]{1,0:T(8,128)(2,1)} %concatenate.3, s32[2048]{0:T(1024)S(1)} %pad_clamp_fusion), kind=kCustom, calls=%fused_computation | custom fusion | bytes 9441792 | tf_op jit(solution)/shard_map/gather | solution.py:127
  102.9 108.9 %all_to_all.10 = bf16[16,72,2048]{2,1,0:T(8,128)(2,1)S(1)} all-to-all(bf16[16,72,2048]{2,1,0:T(8,128)(2,1)} %bitcast.93), channel_id=1, replica_groups=mesh['groups'=2,'wide'=16] {'wide'}, dimensions={0} | all-to-all | bytes 9437184 | tf_op jit(solution)/shard_map/all_to_all | solution.py:128
  211.8 3.9 %fusion.18 = f32[1152,768]{1,0:T(8,128)S(1)} fusion(bf16[1152,2048]{1,0:T(8,128)(2,1)S(1)} %bitcast.100, bf16[1,2048,768]{2,1,0:T(8,128)(2,1)S(1)} %copy-done.8), kind=kOutput, calls=%fused_computation.29 | convolution fusion | flops 3623878656 | bytes 11403264 | tf_op jit(solution)/shard_map/dot_general | solution.py:65
  215.7 4.2 %fusion.15 = bf16[1152,768]{1,0:T(8,128)(2,1)S(1)} fusion(bf16[1152,2048]{1,0:T(8,128)(2,1)S(1)} %bitcast.101, f32[1152,768]{1,0:T(8,128)S(1)} %fusion.18, bf16[1,2048,768]{2,1,0:T(8,128)(2,1)S(1)} %copy-done.9), kind=kOutput, calls=%fused_computation.26 | convolution fusion | flops 3629187072 | bytes 13172736 | tf_op jit(solution)/shard_map/dot_general | solution.py:66
  219.9 5.5 %convolution_convert_fusion = bf16[1152,2048]{1,0:T(8,128)(2,1)} fusion(bf16[1152,768]{1,0:T(8,128)(2,1)S(1)} %fusion.15, bf16[1,768,2048]{2,1,0:T(8,128)(2,1)S(1)} %copy-done), kind=kOutput, calls=%fused_computation.24 | convolution fusion | flops 3626237952 | bytes 9633792 | tf_op jit(solution)/shard_map/dot_general | solution.py:68
  225.5 4.9 %all-to-all-start.1 = ((bf16[16,72,2048]{2,1,0:T(8,128)(2,1)}), bf16[16,72,2048]{2,1,0:T(8,128)(2,1)}, u32[]{:S(2)}, u32[]{:S(2)}) async-start(bf16[16,72,2048]{2,1,0:T(8,128)(2,1)} %bitcast.99), calls=%async_computation.1 | async-start | bytes 9437184 | tf_op jit(solution)/shard_map/all_to_all | solution.py:130
  230.6 103.6 %all-to-all-done.1 = bf16[16,72,2048]{2,1,0:T(8,128)(2,1)} async-done(((bf16[16,72,2048]{2,1,0:T(8,128)(2,1)}), bf16[16,72,2048]{2,1,0:T(8,128)(2,1)}, u32[]{:S(2)}, u32[]{:S(2)}) %all-to-all-start.1) | async-done | bytes 4718624 | tf_op jit(solution)/shard_map/all_to_all | solution.py:130
  334.1 11.8 %gather_fusion.1 = bf16[1024,2048]{1,0:T(8,128)(2,1)} fusion(bf16[1152,2048]{1,0:T(8,128)(2,1)} %bitcast.24, s32[1024]{0:T(1024)S(1)} %broadcast_clamp_fusion), kind=kCustom, calls=%fused_computation.1 | custom fusion | bytes 8392704 | tf_op jit(solution)/shard_map/gather | solution.py:131
  345.9 6.6 %fusion.14 = f32[128,2048]{1,0:T(8,128)S(1)} fusion(bf16[1024,2048]{1,0:T(8,128)(2,1)} %gather_fusion.1, f32[128,8]{1,0:T(8,128)S(1)} %copy.39), kind=kLoop, calls=%fused_computation.23 | loop fusion | flops 6029312 | bytes 5246976 | tf_op jit(solution)/shard_map/reduce_sum | solution.py:133
  352.5 0.9 add_convert_fusion
  (62 shorter events, 1.4 us)
Async XLA Ops:
  6.5 213.4 %copy-start = (bf16[1,768,2048]{2,1,0:T(8,128)(2,1)S(1)}, bf16[1,768,2048]{2,1,0:T(8,128)(2,1)}, u32[]{:S(2)}) copy-start(bf16[1,768,2048]{2,1,0:T(8,128)(2,1)} %param.29) | copy-start | bytes 9437188
  6.5 77.7 %all-gather.2.cloned.1.call-start = ((), (), s32[]{:S(2)}) async-start(), calls=%async_computation.2 | async-start | bytes 8912896 | tf_op jit(solution)/shard_map/all_gather | solution.py:110
  24.0 30.0 %copy-start.5 = (s32[128,8]{0,1:T(8,128)S(1)}, s32[128,8]{0,1:T(8,128)}, u32[]{:S(2)}) copy-start(s32[128,8]{0,1:T(8,128)} %param.25) | copy-start | bytes 12292
  25.7 3.2 copy-start.3
  30.5 1.0 copy-start.4
  33.2 3.2 copy-start.3
  38.0 1.0 copy-start.4
  40.8 3.2 copy-start.3
  45.5 1.0 copy-start.4
  84.2 5.9 %copy-start.7 = (f32[2048]{0:T(1024)S(1)}, f32[2048]{0:T(1024)}, u32[]{:S(2)}) copy-start(f32[2048]{0:T(1024)} %param.24) | copy-start | bytes 24580
  89.1 1.0 copy-start.1
  102.9 108.9 %copy-start.8 = (bf16[1,2048,768]{2,1,0:T(8,128)(2,1)S(1)}, bf16[1,2048,768]{2,1,0:T(8,128)(2,1)}, u32[]{:S(2)}) copy-start(bf16[1,2048,768]{2,1,0:T(8,128)(2,1)} %param.27) | copy-start | bytes 9437188
  211.8 3.9 %copy-start.9 = (bf16[1,2048,768]{2,1,0:T(8,128)(2,1)S(1)}, bf16[1,2048,768]{2,1,0:T(8,128)(2,1)}, u32[]{:S(2)}) copy-start(bf16[1,2048,768]{2,1,0:T(8,128)(2,1)} %param.28) | copy-start | bytes 9437188
  225.5 4.9 %copy-start.6 = (f32[128,8]{0,1:T(8,128)S(1)}, f32[128,8]{0,1:T(8,128)}, u32[]{:S(2)}) copy-start(f32[128,8]{0,1:T(8,128)} %param.26) | copy-start | bytes 12292
  225.5 108.6 %all-to-all-start.1 = ((bf16[16,72,2048]{2,1,0:T(8,128)(2,1)}), bf16[16,72,2048]{2,1,0:T(8,128)(2,1)}, u32[]{:S(2)}, u32[]{:S(2)}) async-start(bf16[16,72,2048]{2,1,0:T(8,128)(2,1)} %bitcast.99), calls=%async_computation.1 | async-start | bytes 9437184 | tf_op jit(solution)/shard_map/all_to_all | solution.py:130
  345.9 6.6 %copy-start.2 = (f32[128,2048]{1,0:T(8,128)S(1)}, f32[128,2048]{1,0:T(8,128)}, u32[]{:S(2)}) copy-start(f32[128,2048]{1,0:T(8,128)} %copy-done.1) | copy-start | bytes 3145732
Sparse Core Ops, SparseCore 0:
  9.5 74.6 all-gather.1
where the time goes:
time: 361 us; the launch traced here: 360 us
  waiting for transfers between devices  128 us (35%)
  blocking collectives  109 us (30%)
  local copies, waits for them, and re-layouts  52.1 us (14%)
  matrix products  32.8 us (9%)
  other arithmetic  19.5 us (5%)
  between operations  14.3 us (4%)
  starting transfers between devices  4.93 us (1%)
    all_to_all x1, blocking collectives, per_device(): lax.all_to_all(outgoing, 'wide', split_axis=0, concat_axis=0, tiled=True)  109 us
    all_to_all x1, waiting for transfers between devices, per_device(): lax.all_to_all(served, 'wide', split_axis=0, concat_axis=0, tiled=True)  104 us
    all_gather x1, waiting for transfers between devices, per_device(): lax.all_gather(o_weight, 'wide', axis=0, tiled=True)  23.3 us
    gather x1, local copies, waits for them, and re-layouts, per_device(): returned_rows.reshape(devices * capacity, D)[slot_index]  11.8 us
    gather x1, local copies, waits for them, and re-layouts, per_device(): outgoing = padded[slot_token].reshape(devices, capacity, D)  11.8 us
    unnamed x20, local copies, waits for them, and re-layouts  8.47 us
    dot_general x4, matrix products, update(): jnp.einsum('tgrd,kgd->grtk', query_four, key_three, preferred_element_typ...  7.96 us
  transfers between devices with their start and end apart: 2, of which 2 were waited for; matrix products, arithmetic and copies ran while one was open for 14% of the time, Pallas kernels for 0%

commit v1 on v0

v1 whole, which is shorter than its diff:
```python
import functools
import jax
import jax.numpy as jnp
from jax import lax
from jax.experimental import pallas as pl
from jax.experimental.pallas import tpu as pltpu
from jax.sharding import PartitionSpec as P

D = 2048
HEADS = 16
KV_HEADS = 2
HEAD = 128
TOPK = 8
SPAN = 128
PACK = 2
EXP2_SCALE = HEAD ** (-0.5) * 1.4426950408889634
CHUNKS = 2


def attention_kernel(length_ref, q_ref, nk_ref, nv_ref, k_ref, v_ref, out_ref):
    tokens = q_ref.shape[0]
    rows = PACK * tokens
    cache = k_ref.shape[1]
    q = jnp.concatenate([q_ref[:, i * HEAD : (i + 1) * HEAD] for i in range(PACK)], axis=0)
    dims = (((1,), (1,)), ((), ()))
    s = lax.dot_general(q, k_ref[0], dims, preferred_element_type=jnp.float32)
    position = lax.broadcasted_iota(jnp.int32, (1, cache), 1)
    s = jnp.where(position < length_ref[0], s, jnp.float32(-1e30))
    s_new = lax.dot_general(q, nk_ref[...], dims, preferred_element_type=jnp.float32)
    row = lax.broadcasted_iota(jnp.int32, (rows, tokens), 0) % tokens
    column = lax.broadcasted_iota(jnp.int32, (rows, tokens), 1)
    s_new = jnp.where(column <= row, s_new, jnp.float32(-1e30))
    top = jnp.maximum(jnp.max(s, axis=1, keepdims=True), jnp.max(s_new, axis=1, keepdims=True))
    w = jnp.exp2((s - top) * EXP2_SCALE)
    w_new = jnp.exp2((s_new - top) * EXP2_SCALE)
    total = jnp.sum(w, axis=1, keepdims=True) + jnp.sum(w_new, axis=1, keepdims=True)
    out = jnp.dot(w.astype(jnp.bfloat16), v_ref[0], preferred_element_type=jnp.float32)
    out += jnp.dot(w_new.astype(jnp.bfloat16), nv_ref[...], preferred_element_type=jnp.float32)
    out = (out / total).astype(out_ref.dtype)
    for i in range(PACK):
        out_ref[:, i * HEAD : (i + 1) * HEAD] = out[i * tokens : (i + 1) * tokens]


def attention(length, queries, new_keys, new_values, cache_keys, cache_values):
    tokens, width = queries.shape
    cache = cache_keys.shape[1]
    per_group = HEADS // KV_HEADS // PACK
    return pl.pallas_call(
        attention_kernel,
        grid=(HEADS // PACK,),
        in_specs=[
            pl.BlockSpec(memory_space=pltpu.SMEM),
            pl.BlockSpec((tokens, PACK * HEAD), lambda i: (0, i)),
            pl.BlockSpec((tokens, HEAD), lambda i: (0, i // per_group)),
            pl.BlockSpec((tokens, HEAD), lambda i: (0, i // per_group)),
            pl.BlockSpec((1, cache, HEAD), lambda i: (0, 0, i // per_group)),
            pl.BlockSpec((1, cache, HEAD), lambda i: (0, 0, i // per_group)),
        ],
        out_specs=pl.BlockSpec((tokens, PACK * HEAD), lambda i: (0, i)),
        out_shape=jax.ShapeDtypeStruct((tokens, width), jnp.bfloat16),
        cost_estimate=pl.CostEstimate(
            flops=4 * tokens * width * (cache + tokens),
            bytes_accessed=4 * cache * KV_HEADS * HEAD + 4 * tokens * width,
            transcendentals=tokens * HEADS * (cache + tokens),
        ),
    )(length, queries, new_keys, new_values, cache_keys, cache_values)


def run_expert(rows_in, gate_w, up_w, down_w):
    gate_part = jnp.dot(rows_in, gate_w, preferred_element_type=jnp.float32)
    up_part = jnp.dot(rows_in, up_w, preferred_element_type=jnp.float32)
    activated = (jax.nn.silu(gate_part) * up_part).astype(jnp.bfloat16)
    return jnp.dot(activated, down_w, preferred_element_type=jnp.float32)


def sparse_experts(normed, expert_ids, shares, gate_w, up_w, down_w, devices):
    token_count = normed.shape[0]
    capacity = SPAN * TOPK // devices + max(2, SPAN * TOPK // (8 * devices))
    flat_ids = expert_ids.reshape(-1)
    one_hot = (flat_ids[:, None] == jnp.arange(devices, dtype=jnp.int32)[None, :]).astype(jnp.int32)
    ranks = jnp.sum(jnp.cumsum(one_hot, axis=0) * one_hot, axis=1) - 1
    slot_index = flat_ids * capacity + ranks
    token_of = jnp.arange(flat_ids.shape[0], dtype=jnp.int32) // TOPK
    slot_token = (
        jnp.full((devices * capacity,), token_count, jnp.int32).at[slot_index].set(token_of)
    )
    padded = jnp.concatenate([normed, jnp.zeros((1, D), jnp.bfloat16)], axis=0)
    outgoing = padded[slot_token].reshape(devices, capacity, D)
    arrived = lax.all_to_all(outgoing, "wide", split_axis=0, concat_axis=0, tiled=True)
    served = run_expert(arrived.reshape(-1, D), gate_w, up_w, down_w).astype(jnp.bfloat16)
    served = served.reshape(devices, capacity, D)
    returned_rows = lax.all_to_all(served, "wide", split_axis=0, concat_axis=0, tiled=True)
    picked = returned_rows.reshape(devices * capacity, D)[slot_index].reshape(token_count, TOPK, D)
    return jnp.sum(picked.astype(jnp.float32) * shares[..., None], axis=1)


def dense_experts(normed, expert_ids, shares, gate_w, up_w, down_w, devices):
    token_count = normed.shape[0]
    me = lax.axis_index("wide")
    hits = expert_ids[:, :, None] == jnp.arange(devices, dtype=jnp.int32)[None, None, :]
    share_of = jnp.sum(jnp.where(hits, shares[..., None], 0.0), axis=1)
    all_shares = lax.all_gather(share_of, "wide", axis=0, tiled=False)
    mine = lax.dynamic_index_in_dim(all_shares, me, axis=2, keepdims=False)
    size = token_count // CHUNKS
    parts = []
    for c in range(CHUNKS):
        piece = lax.slice_in_dim(normed, c * size, (c + 1) * size, axis=0)
        rows = lax.all_gather(piece, "wide", axis=0, tiled=True)
        out = run_expert(rows, gate_w, up_w, down_w)
        scale = mine[:, c * size : (c + 1) * size].reshape(-1, 1)
        scaled = (out * scale).astype(jnp.bfloat16)
        parts.append(lax.psum_scatter(scaled, "wide", scatter_dimension=0, tiled=True))
    return jnp.concatenate(parts, axis=0).astype(jnp.float32)


def per_device(
    residual,
    queries,
    new_keys,
    new_values,
    cache_keys,
    cache_values,
    cache_len,
    o_weight,
    norm_gain,
    expert_ids,
    gate_raw,
    w_gate,
    w_up,
    w_down,
):
    devices = lax.axis_size("wide")
    me = lax.axis_index("wide")
    length = lax.dynamic_slice_in_dim(cache_len, me, 1, 0)
    attn = attention(length, queries, new_keys, new_values, cache_keys, cache_values)
    projected = jnp.dot(
        attn,
        lax.all_gather(o_weight, "wide", axis=0, tiled=True),
        preferred_element_type=jnp.float32,
    )
    mixed = residual.astype(jnp.float32) + projected
    normed = (
        mixed * lax.rsqrt(jnp.mean(mixed * mixed, axis=-1, keepdims=True) + 1e-06) * norm_gain
    ).astype(jnp.bfloat16)
    shares = gate_raw / jnp.sum(gate_raw, axis=-1, keepdims=True)
    experts = dense_experts if devices <= 2 * TOPK else sparse_experts
    routed = experts(normed, expert_ids, shares, w_gate[0], w_up[0], w_down[0], devices)
    return (mixed + routed).astype(jnp.bfloat16)


def solution(mesh):
    rows = P(("groups", "wide"), None)
    blocks = P(("groups", "wide"), None, None)
    weights = P("wide", None, None)
    placed = (rows, rows, rows, rows, blocks, blocks, P("groups"), P("wide", None), P())
    placed += (rows, rows, weights, weights, weights)
    return jax.shard_map(
        per_device,
        mesh=mesh,
        in_specs=placed,
        out_specs=rows,
        check_vma=False,
    )
```

time: 361 us -> 354 us (0.981)
  the two profiles are of different devices: /device:TPU:13 before, /device:TPU:0 now
where the time goes in v1:
time: 354 us; the launch traced here: 353 us
  waiting for transfers between devices  255 us (72%)
  matrix products  46.5 us (13%)
  blocking collectives  19.5 us (6%)
  between operations  13.2 us (4%)
  Pallas kernels  13 us (4%)
    reduce_scatter x2, waiting for transfers between devices, dense_experts(): lax.psum_scatter(scaled, 'wide', scatter_dimension=0, tiled=True)  130 us
    all_gather x1, waiting for transfers between devices, per_device(): lax.all_gather(o_weight, 'wide', axis=0, tiled=True)  64.8 us
    all_gather x2, waiting for transfers between devices, dense_experts(): rows = lax.all_gather(piece, 'wide', axis=0, tiled=True)  59 us
    dot_general x2, matrix products, run_expert(): return jnp.dot(activated, down_w, preferred_element_type=jnp.float32)  25.1 us
    all_gather x1, blocking collectives, dense_experts(): all_shares = lax.all_gather(share_of, 'wide', axis=0, tiled=False)  19.5 us
    dot_general x2, matrix products, run_expert(): up_part = jnp.dot(rows_in, up_w, preferred_element_type=jnp.float32)  16.4 us
    pallas_call x1, Pallas kernels, attention(): pl.pallas_call(attention_kernel, grid=(HEADS // PACK,), in_specs=[pl.Bloc...  13 us
  transfers between devices with their start and end apart: 5, of which 5 were waited for; matrix products, arithmetic and copies ran while one was open for 12% of the time, Pallas kernels for 4%

profile of v1, /device:TPU:0, one launch (start us, length us, event | category | flops | bytes accessed | tf_op | source)
XLA Modules:
  0.0 353.4 jit_solution(15135858083347969292)
XLA Ops:
  6.5 0.0 copy-start
  6.5 0.0 all-gather.5.cloned.1.call-start
  6.5 0.7 all-gather.5.cloned.1.call-update
  7.3 0.0 all-gather.7.cloned.1.call-start
  7.3 1.4 dynamic_slice.7.length_ref
  8.8 13.0 %shard_map.136 = bf16[128,2048]{1,0:T(8,128)(2,1)} custom-call(s32[1]{0:T(128)} %dynamic_slice.7.length_ref, bf16[128,2048]{1,0:T(8,128)(2,1)} %q_ref.1, bf16[128,256]{1,0:T(8,128)(2,1)} %nk_ref.1, bf16[128,256]{1,0:T(8,128)(2,1)} %nv_ref.1, bf16[1,2048,256]{2,1,0:T(8,128)(2,1)} %k_ref.1, bf16[1,2048,256]{2,1,0:T(8,128)(2,1)} %v_ref.1), custom_call_target="tpu_custom_call" | custom-call | flops 2281701376 | bytes 3145728 | tf_op jit(solution)/shard_map/pallas_call | solution.py:48
  21.7 0.0 copy-start.3
  21.7 64.8 %all-gather.5.cloned.1.call-done = bf16[2048,2048]{1,0:T(8,128)(2,1)} async-done(((bf16[128,2048]{1,0:T(8,128)(2,1)}), bf16[2048,2048]{1,0:T(8,128)(2,1)}) %all-gather.5.cloned.1.call-update) | async-done | bytes 8388624 | tf_op jit(solution)/shard_map/all_gather | solution.py:138
  86.5 5.0 %multiply_reduce_fusion = (f32[128]{0:T(128)S(1)}, f32[128,2048]{1,0:T(8,128)S(1)}) fusion(bf16[128,2048]{1,0:T(8,128)(2,1)} %shard_map.136, bf16[2048,2048]{1,0:T(8,128)(2,1)} %all-gather.5.cloned.1.call-done, bf16[128,2048]{1,0:T(8,128)(2,1)} %param.14), kind=kOutput, calls=%fused_computation.17 | convolution fusion | flops 1074790272 | bytes 10486272 | tf_op jit(solution)/shard_map/dot_general | solution.py:136
  91.5 0.0 copy-start.1
  91.5 0.0 copy-start.2
  91.5 0.0 copy-start.4
  91.6 0.9 copy-done.1
  92.5 0.0 copy-done.3
  92.5 0.2 multiply_convert_fusion.4
  92.7 0.9 fusion.20
  93.5 0.0 all-gather.7.cloned.1.call-update
  93.5 0.0 all-gather.9.cloned.1.call-start
  93.6 0.7 all-gather.9.cloned.1.call-update
  94.3 0.0 reduce-scatter.3.cloned.1.call-start
  94.3 0.0 copy-done.2
  94.4 0.0 copy-done.4
  94.4 19.5 %all-gather = f32[2048,16]{0,1:T(8,128)S(1)} all-gather(f32[128,16]{0,1:T(8,128)S(1)} %select_reduce_fusion), channel_id=2, replica_groups=mesh['groups'=2,'wide'=16] {'wide'}, dimensions={0}, use_global_device_ids=true | all-gather | bytes 139264 | tf_op jit(solution)/shard_map/all_gather | solution.py:102
  113.9 0.1 fusion.21
  114.0 0.1 mul.59
  114.0 28.8 %all-gather.7.cloned.1.call-done = bf16[1024,2048]{1,0:T(8,128)(2,1)} async-done(((bf16[64,2048]{1,0:T(8,128)(2,1)}), bf16[1024,2048]{1,0:T(8,128)(2,1)}) %all-gather.7.cloned.1.call-update) | async-done | bytes 4194320 | tf_op jit(solution)/shard_map/all_gather | solution.py:108
  142.9 8.2 %fusion.4 = f32[1024,768]{1,0:T(8,128)} fusion(bf16[1024,2048]{1,0:T(8,128)(2,1)} %all-gather.7.cloned.1.call-done, bf16[1,2048,768]{2,1,0:T(8,128)(2,1)} %param.26), kind=kOutput, calls=%fused_computation.6 | convolution fusion | flops 3221225472 | bytes 10485760 | tf_op jit(solution)/shard_map/dot_general | solution.py:71
  151.1 0.0 copy-done
  151.1 12.4 %multiply_convert_fusion.1 = bf16[1024,2048]{1,0:T(8,128)(2,1)} fusion(f32[1024]{0:T(1024)S(1)} %mul.59, bf16[1,768,2048]{2,1,0:T(8,128)(2,1)S(1)} %copy-done, f32[1024,768]{1,0:T(8,128)} %fusion.4, bf16[1024,2048]{1,0:T(8,128)(2,1)} %all-gather.7.cloned.1.call-done, bf16[1,2048,768]{2,1,0:T(8,128)(2,1)} %param.25), kind=kOutput, calls=%fused_computation.1 | convolution fusion | flops 6451363840 | bytes 17829888 | tf_op jit(solution)/shard_map/dot_general | solution.py:73
  163.5 0.0 reduce-scatter.3.cloned.1.call-update
  163.5 0.2 reduce-scatter.5.cloned.1.call-start
  163.7 0.1 mul.64
  163.8 30.2 %all-gather.9.cloned.1.call-done = bf16[1024,2048]{1,0:T(8,128)(2,1)} async-done(((bf16[64,2048]{1,0:T(8,128)(2,1)}), bf16[1024,2048]{1,0:T(8,128)(2,1)}) %all-gather.9.cloned.1.call-update) | async-done | bytes 4194320 | tf_op jit(solution)/shard_map/all_gather | solution.py:108
  194.0 8.2 %fusion.2 = f32[1024,768]{1,0:T(8,128)} fusion(bf16[1024,2048]{1,0:T(8,128)(2,1)} %all-gather.9.cloned.1.call-done, bf16[1,2048,768]{2,1,0:T(8,128)(2,1)} %param.26), kind=kOutput, calls=%fused_computation.4 | convolution fusion | flops 3221225472 | bytes 10485760 | tf_op jit(solution)/shard_map/dot_general | solution.py:71
  202.2 12.7 %multiply_convert_fusion = bf16[1024,2048]{1,0:T(8,128)(2,1)} fusion(f32[1024]{0:T(1024)S(1)} %mul.64, bf16[1,768,2048]{2,1,0:T(8,128)(2,1)S(1)} %copy-done, f32[1024,768]{1,0:T(8,128)} %fusion.2, bf16[1024,2048]{1,0:T(8,128)(2,1)} %all-gather.9.cloned.1.call-done, bf16[1,2048,768]{2,1,0:T(8,128)(2,1)} %param.25), kind=kOutput, calls=%fused_computation | convolution fusion | flops 6451363840 | bytes 17829888 | tf_op jit(solution)/shard_map/dot_general | solution.py:73
  214.9 0.0 reduce-scatter.5.cloned.1.call-update
  214.9 54.1 %reduce-scatter.3.cloned.1.call-done = bf16[64,2048]{1,0:T(8,128)(2,1)} async-done(((bf16[1024,2048]{1,0:T(8,128)(2,1)}), bf16[64,2048]{1,0:T(8,128)(2,1)}) %reduce-scatter.3.cloned.1.call-update) | async-done | bytes 262160 | tf_op jit(solution)/shard_map/reduce_scatter | solution.py:112
  269.1 75.6 %reduce-scatter.5.cloned.1.call-done = bf16[64,2048]{1,0:T(8,128)(2,1)} async-done(((bf16[1024,2048]{1,0:T(8,128)(2,1)}), bf16[64,2048]{1,0:T(8,128)(2,1)}) %reduce-scatter.5.cloned.1.call-update) | async-done | bytes 262160 | tf_op jit(solution)/shard_map/reduce_scatter | solution.py:112
  344.6 2.2 add_convert_fusion
  (6 shorter events, 0.1 us)
Async XLA Ops:
  6.5 144.6 %copy-start = (bf16[1,768,2048]{2,1,0:T(8,128)(2,1)S(1)}, bf16[1,768,2048]{2,1,0:T(8,128)(2,1)}, u32[]{:S(2)}) copy-start(bf16[1,768,2048]{2,1,0:T(8,128)(2,1)} %param.27) | copy-start | bytes 9437188
  6.5 80.0 %all-gather.5.cloned.1.call-start = ((), (), s32[]{:S(2)}) async-start(), calls=%async_computation.2 | async-start | bytes 8912896 | tf_op jit(solution)/shard_map/all_gather | solution.py:138
  7.3 135.6 %all-gather.7.cloned.1.call-start = ((), (), s32[]{:S(2)}) async-start(), calls=%async_computation.3 | async-start | bytes 4456448 | tf_op jit(solution)/shard_map/all_gather | solution.py:108
  21.7 70.8 %copy-start.3 = (f32[2048]{0:T(1024)S(1)}, f32[2048]{0:T(1024)}, u32[]{:S(2)}) copy-start(f32[2048]{0:T(1024)} %param.22) | copy-start | bytes 24580
  91.5 1.0 copy-start.1
  91.5 2.8 copy-start.2
  91.5 2.8 copy-start.4
  93.5 100.4 %all-gather.9.cloned.1.call-start = ((), (), s32[]{:S(2)}) async-start(), calls=%async_computation.5 | async-start | bytes 4456448 | tf_op jit(solution)/shard_map/all_gather | solution.py:108
  94.3 174.8 %reduce-scatter.3.cloned.1.call-start = ((), (), s32[]{:S(2)}) async-start(), calls=%async_computation.4 | async-start | bytes 4456448 | tf_op jit(solution)/shard_map/reduce_scatter | solution.py:112
  163.5 181.1 %reduce-scatter.5.cloned.1.call-start = ((), (), s32[]{:S(2)}) async-start(), calls=%async_computation.6 | async-start | bytes 4456448 | tf_op jit(solution)/shard_map/reduce_scatter | solution.py:112
Sparse Core Ops, SparseCore 0:
  9.5 77.0 all-gather.4
  93.7 49.1 all-gather.6
  145.1 48.8 all-gather.8
  197.7 71.2 reduce-scatter.2
  272.8 71.8 reduce-scatter.4
